TPU v7x, 128 devices: a whole 4x4x4 slice. The times are simulated.
128 devices in a mesh: view: 4 (over x), xy: 16 (over z, y), gz: 2 (over core).
Axes of the slice: x: 4, y: 4, z: 4, core: 2. Of those that a mesh axis runs over, the one named last changes fastest.
Arguments:
- estimate: float32 [64, 1024, 128], P('gz', 'xy'), may hold values from 0.5 to 2
- views: bfloat16 [4, 64, 1024, 128], P('view', 'gz', 'xy'), may hold values from 0.19921875 to 3
- shifts: int32 [4, 3], P('view'), may hold values from -32 to 32, as said below
- kernels: float32 [4, 3, 63], P('view'), may hold values from 0.02 to 1
- coverage: int32 [4, 8, 1], replicated, may hold values from 0 to 1, as said below
Outputs:
- refined: float32 [64, 1024, 128], P('gz', 'xy')
Inputs may be any that keep to these rules, and one draw needn't show every extreme that they name: `shifts`: both ends -32 and 32 occur in every draw. `coverage`: every block is covered by at least one view.
All inputs are finite; a program needn't handle non-finite values.
Results may differ from a plain program's by a relative error of at most 0.0003.
Values may be sent and summed in bfloat16 or wider, within the bound.
No kernel may reach another device: no remote copies, remote signals or barrier semaphores. Data moves between devices by JAX's collectives and lax.ppermute only.
A program may use at most 64 MiB of HBM per device.

v0:
```python
import jax
import jax.numpy as jnp
from jax import lax
from jax.sharding import PartitionSpec as P

SHIFT = 32
BLOCK = 128
ITERS = 2


def shortened(shard):

    def short(part):
        return part.astype(jnp.bfloat16) if part.dtype == jnp.float32 else part

    return jax.tree.map(short, shard)


def extended(cells, sides, width):
    for axis, dim in sides:
        count = lax.axis_size(axis)
        ends = count - 1
        head = lax.slice_in_dim(cells, 0, width, axis=dim)
        tail = lax.slice_in_dim(cells, cells.shape[dim] - width, cells.shape[dim], axis=dim)
        cells = jnp.concatenate(
            [
                lax.ppermute(tail, axis, [(i, (i + 1) % count) for i in range(ends)]),
                cells,
                lax.ppermute(head, axis, [((i + 1) % count, i) for i in range(ends)]),
            ],
            axis=dim,
        )
    return cells


def band(kern, rows, cols, offset):
    row_ids = lax.broadcasted_iota(jnp.int32, (rows, cols), 0)
    col_ids = lax.broadcasted_iota(jnp.int32, (rows, cols), 1)
    offsets = row_ids - col_ids + offset

    def add_tap(tap_index, summed):
        return summed + jnp.where(offsets == tap_index, kern[tap_index], 0.0)

    return lax.fori_loop(0, kern.shape[0], add_tap, jnp.zeros((rows, cols), jnp.float32))


def along_x(vol, matrix):
    return jnp.einsum("zyx,xk->zyk", vol, matrix, precision=lax.Precision.HIGHEST)


def banded_rows(piece, matrix, half):
    rows_all = piece.shape[1]
    tile = matrix.shape[1]
    padded = jnp.pad(piece, ((0, 0), (half, half), (0, 0)))
    blocks = rows_all // tile
    windows = jnp.stack(
        [
            lax.slice_in_dim(padded, b * tile, b * tile + tile + 2 * half, axis=1)
            for b in range(blocks)
        ],
        axis=1,
    )
    out = jnp.einsum("zbwx,wk->zbkx", windows, matrix, precision=lax.Precision.HIGHEST)
    return out.reshape(piece.shape[0], rows_all, piece.shape[2])


def along_rows(vol, pencil_mat, half):
    out = banded_rows(
        lax.all_to_all(shortened(vol), "xy", split_axis=0, concat_axis=1, tiled=True).astype(
            vol.dtype
        ),
        pencil_mat,
        half,
    )
    return lax.all_to_all(out, "xy", split_axis=1, concat_axis=0, tiled=True)


def along_planes(vol, matrix, half):
    padded = extended(vol, (("gz", 0),), half)
    return jnp.einsum("zyx,zk->kyx", padded, matrix, precision=lax.Precision.HIGHEST)


def on_device(estimate, views, shifts, kernels, coverage):
    slab, strip, width = estimate.shape
    taps = kernels.shape[2]
    half = (taps - 1) // 2
    tile = 128
    psf = kernels[0] / jnp.sum(kernels[0], axis=1, keepdims=True)
    raw = views[0]
    margin = SHIFT
    padded = extended(raw, (("gz", 0), ("xy", 1)), margin)
    padded = jnp.pad(padded, ((0, 0), (0, 0), (margin, margin)))
    start = margin + shifts[0]
    data = lax.dynamic_slice(padded, (start[0], start[1], start[2]), (slab, strip, width)).astype(
        jnp.float32
    )
    field = estimate
    row_first = lax.axis_index("xy") * strip
    planes = field.shape[0]
    mats = []
    for reverse in (False, True):
        rows_psf = psf[:, ::-1] if reverse else psf
        x_mat = band(rows_psf[2], width, width, half)
        z_mat = band(rows_psf[0], planes + 2 * half, planes, 0)
        y_mat = band(rows_psf[1], tile + 2 * half, tile, 0)
        mats.append((x_mat, y_mat, None, z_mat))
    row_global = row_first + lax.broadcasted_iota(jnp.int32, (strip,), 0)
    row_onehot = (row_global[:, None] // BLOCK == jnp.arange(coverage.shape[1])[None]).astype(
        jnp.float32
    )
    col_onehot = (
        jnp.arange(width)[:, None] // BLOCK == jnp.arange(coverage.shape[2])[None]
    ).astype(jnp.float32)
    grid = jnp.einsum("vbc,yb,xc->vyx", coverage.astype(jnp.float32), row_onehot, col_onehot)
    mine = lax.dynamic_index_in_dim(grid, lax.axis_index("view"), 0, keepdims=False)
    count = jnp.sum(grid, axis=0)
    for step in range(ITERS):
        predicted = along_x(field, mats[0][0])
        predicted = along_rows(predicted, mats[0][1], half)
        predicted = along_planes(predicted, mats[0][3], half)
        ratio = data / (predicted + 0.05)
        back = along_x(ratio, mats[1][0])
        back = along_rows(back, mats[1][1], half)
        back = along_planes(back, mats[1][3], half)
        term = mine[None] * back
        total = lax.psum(term, "view")
        field = field * total / count[None]
    return field


def solution(mesh):
    placed = (
        P("gz", "xy", None),
        P("view", "gz", "xy", None),
        P("view", None),
        P("view", None, None),
        P(),
    )
    return jax.shard_map(
        on_device, mesh=mesh, in_specs=placed, out_specs=P("gz", "xy", None), check_vma=False
    )
```

profile of v0, /device:TPU:0, one launch (start us, length us, event | category | flops | bytes accessed | tf_op | source)
XLA Modules:
  0.0 838.2 jit_solution(7142134574936693897)
XLA Ops:
  6.5 1.5 copy.224
  8.0 1.3 collective-permute-start.1
  9.3 3.9 collective-permute-start
  14.7 86.1 %while.88 = (s32[]{:T(128)}, f32[128,128]{1,0:T(8,128)S(1)}, f32[63]{0:T(128)S(1)}, s32[]{:T(128)}, s32[]{:T(128)}) while((s32[]{:T(128)}, f32[128,128]{1,0:T(8,128)S(1)}, f32[63]{0:T(128)S(1)}, s32[]{:T(128)}, s32[]{:T(128)}) %tuple.181), condition=%wide.region_10.11_spmd.clone, body=%wide.region_9.10_spmd.clone.sunk | while | flops 98307 | bytes 131171 | solution.py:44
  100.9 1.8 fusion.48
  102.6 8.2 all-to-all-start
  110.8 87.1 %while.87 = (s32[]{:T(128)}, f32[190,128]{1,0:T(8,128)S(1)}, f32[63]{0:T(128)S(1)}, s32[]{:T(128)}, s32[]{:T(128)}) while((s32[]{:T(128)}, f32[190,128]{1,0:T(8,128)S(1)}, f32[63]{0:T(128)S(1)}, s32[]{:T(128)}, s32[]{:T(128)}) %tuple.184), condition=%wide.region_8.9_spmd.clone, body=%wide.region_7.8_spmd.clone.sunk | while | flops 121603 | bytes 194659 | solution.py:44
  198.1 86.6 %while.89 = (s32[]{:T(128)}, f32[128,128]{1,0:T(8,128)S(1)}, f32[63]{0:T(128)S(1)}, s32[]{:T(128)}, s32[]{:T(128)}) while((s32[]{:T(128)}, f32[128,128]{1,0:T(8,128)S(1)}, f32[63]{0:T(128)S(1)}, s32[]{:T(128)}, s32[]{:T(128)}) %tuple.205), condition=%wide.region_12.13_spmd.clone, body=%wide.region_11.12_spmd.clone.sunk | while | flops 98307 | bytes 131171 | solution.py:44
  286.2 1.8 copy.145
  288.0 7.3 all-to-all-start.1
  295.3 85.6 %while.86 = (s32[]{:T(128)}, f32[94,32]{1,0:T(8,128)S(1)}, f32[63]{0:T(128)S(1)}, s32[]{:T(128)}, s32[]{:T(128)}) while((s32[]{:T(128)}, f32[94,32]{1,0:T(8,128)S(1)}, f32[63]{0:T(128)S(1)}, s32[]{:T(128)}, s32[]{:T(128)}) %tuple.187), condition=%wide.region_6.7_spmd.clone, body=%wide.region_5.6_spmd.clone.sunk | while | flops 15043 | bytes 24163 | solution.py:44
  391.2 5.4 collective-permute-start.2
  397.1 1.3 collective-permute-start.5
  398.4 3.7 collective-permute-start.4
  402.0 1.7 iota_compare_fusion
  403.7 5.6 collective-permute-done.3
  410.5 5.6 fusion.68
  418.0 1.9 convert_divide_fusion.1
  419.9 2.5 convolution_convert_fusion.2
  422.4 9.9 %all-to-all-start.2 = ((bf16[32,64,128]{2,1,0:T(8,128)(2,1)}), bf16[32,64,128]{2,1,0:T(8,128)(2,1)S(1)}, u32[]{:S(2)}, u32[]{:S(2)}) async-start(bf16[32,64,128]{2,1,0:T(8,128)(2,1)} %convolution_convert_fusion.2), calls=%async_computation.2 | async-start | bytes 1048576 | tf_op jit(solution)/shard_map/all_to_all | solution.py:69
  432.3 80.0 %while.85 = (s32[]{:T(128)}, f32[190,128]{1,0:T(8,128)S(1)}, f32[63]{0:T(128)S(1)}, s32[]{:T(128)}, s32[]{:T(128)}) while((s32[]{:T(128)}, f32[190,128]{1,0:T(8,128)S(1)}, f32[63]{0:T(128)S(1)}, s32[]{:T(128)}, s32[]{:T(128)}) %tuple.203), condition=%wide.region_4.5_spmd.clone, body=%wide.region_3.4_spmd.clone.sunk | while | flops 121603 | bytes 194659 | solution.py:44
  513.8 1.8 copy.161
  515.6 7.3 all-to-all-start.3
  523.1 13.8 %all-to-all-done.3 = f32[2,1024,128]{2,0,1:T(2,128)S(1)} async-done(((f32[2,1024,128]{2,0,1:T(2,128)}), f32[2,1024,128]{2,0,1:T(2,128)S(1)}, u32[]{:S(2)}, u32[]{:S(2)}) %all-to-all-start.3) | async-done | bytes 1048608 | tf_op jit(solution)/shard_map/all_to_all | solution.py:75
  538.3 1.3 collective-permute-start.7
  539.6 1.5 copy.163
  541.2 5.0 collective-permute-start.6
  546.1 87.8 %while.84 = (s32[]{:T(128)}, f32[94,32]{1,0:T(8,128)S(1)}, f32[63]{0:T(128)S(1)}, s32[]{:T(128)}, s32[]{:T(128)}) while((s32[]{:T(128)}, f32[94,32]{1,0:T(8,128)S(1)}, f32[63]{0:T(128)S(1)}, s32[]{:T(128)}, s32[]{:T(128)}) %tuple.204), condition=%wide.region_2.3_spmd.clone, body=%wide.region_1.2_spmd.clone.sunk | while | flops 15043 | bytes 24163 | solution.py:44
  634.4 1.8 copy.166
  636.2 1.8 copy.165
  638.0 2.9 fusion.42
  641.0 43.3 %all-reduce.8.cloned.1.call-done = f32[32,64,128]{2,0,1:T(8,128)} async-done(((f32[32,64,128]{2,0,1:T(8,128)}), f32[32,64,128]{2,0,1:T(8,128)}) %all-reduce.8.cloned.1.call-update) | async-done | bytes 1048592 | tf_op jit(solution)/shard_map/psum | solution.py:126
  684.3 1.9 fusion.57
  686.2 1.7 convolution_convert_fusion.1
  687.9 17.1 %all_to_all.108 = bf16[32,64,128]{2,1,0:T(8,128)(2,1)S(1)} all-to-all(bf16[32,64,128]{2,1,0:T(8,128)(2,1)S(1)} %convolution_convert_fusion.1), channel_id=1, replica_groups=mesh['view'=4,'xy'=16,'gz'=2] {'xy'}, dimensions={0} | all-to-all | bytes 1048576 | tf_op jit(solution)/shard_map/all_to_all | solution.py:69
  707.3 17.0 %all_to_all.109 = f32[2,1024,128]{2,0,1:T(2,128)S(1)} all-to-all(f32[2,1024,128]{2,0,1:T(2,128)S(1)} %copy.178), channel_id=1, replica_groups=mesh['view'=4,'xy'=16,'gz'=2] {'xy'}, dimensions={1} | all-to-all | bytes 2097152 | tf_op jit(solution)/shard_map/all_to_all | solution.py:75
  724.7 1.3 collective-permute-start.9
  726.0 3.2 collective-permute-start.8
  731.9 1.9 convert_divide_fusion
  733.9 1.7 convolution_convert_fusion
  735.6 15.0 %all_to_all.110 = bf16[32,64,128]{2,1,0:T(8,128)(2,1)S(1)} all-to-all(bf16[32,64,128]{2,1,0:T(8,128)(2,1)S(1)} %convolution_convert_fusion), channel_id=1, replica_groups=mesh['view'=4,'xy'=16,'gz'=2] {'xy'}, dimensions={0} | all-to-all | bytes 1048576 | tf_op jit(solution)/shard_map/all_to_all | solution.py:69
  752.9 19.9 %all_to_all.111 = f32[2,1024,128]{2,0,1:T(2,128)S(1)} all-to-all(f32[2,1024,128]{2,0,1:T(2,128)S(1)} %copy.194), channel_id=1, replica_groups=mesh['view'=4,'xy'=16,'gz'=2] {'xy'}, dimensions={1} | all-to-all | bytes 2097152 | tf_op jit(solution)/shard_map/all_to_all | solution.py:75
  776.1 3.2 collective-permute-start.10
  779.8 1.5 collective-permute-done.10
  782.0 2.9 fusion.36
  784.9 43.2 %all-reduce.10.cloned.1.call-done = f32[32,64,128]{2,0,1:T(8,128)} async-done(((f32[32,64,128]{2,0,1:T(8,128)}), f32[32,64,128]{2,0,1:T(8,128)}) %all-reduce.10.cloned.1.call-update) | async-done | bytes 1048592 | tf_op jit(solution)/shard_map/psum | solution.py:126
  828.0 1.5 multiply_divide_fusion
  829.5 1.6 copy.201
  (878 shorter events, 531.2 us)
Async XLA Ops:
  6.5 94.3 %copy-start = (f32[32,64,128]{2,1,0:T(8,128)S(1)}, f32[32,64,128]{2,1,0:T(8,128)}, u32[]{:S(2)}) copy-start(f32[32,64,128]{2,1,0:T(8,128)} %param.17) | copy-start | bytes 3145732
  8.0 379.5 %collective-permute-start.1 = (bf16[32,64,128]{2,0,1:T(8,128)(2,1)S(1)}, bf16[32,64,128]{2,0,1:T(8,128)(2,1)S(1)}, u32[]{:S(2)}, u32[]{:S(2)}) collective-permute-start(bf16[32,64,128]{2,0,1:T(8,128)(2,1)S(1)} %bitcast.354), channel_id=1, source_target_pairs={{1,0},{3,2},{5,4},{7,6},{9,8},{11,10},{13,12},{15,14},{17,16},{19,... | collective-permute-start | bytes 1572872 | tf_op jit(solution)/shard_map/ppermute | solution.py:29
  9.3 378.2 %collective-permute-start = (bf16[32,64,128]{2,0,1:T(8,128)(2,1)S(1)}, bf16[32,64,128]{2,0,1:T(8,128)(2,1)}, u32[]{:S(2)}, u32[]{:S(2)}) collective-permute-start(bf16[32,64,128]{2,0,1:T(8,128)(2,1)S(1)} %bitcast.355), channel_id=1, source_target_pairs={{0,1},{2,3},{4,5},{6,7},{8,9},{10,11},{12,13},{14,15},{16,17},{18,... | collective-permute-start | bytes 1572872 | tf_op jit(solution)/shard_map/ppermute | solution.py:27
  102.6 182.0 %all-to-all-start = ((bf16[32,64,128]{2,1,0:T(8,128)(2,1)}), bf16[32,64,128]{2,1,0:T(8,128)(2,1)S(1)}, u32[]{:S(2)}, u32[]{:S(2)}) async-start(bf16[32,64,128]{2,1,0:T(8,128)(2,1)} %fusion.48), calls=%async_computation | async-start | bytes 1048576 | tf_op jit(solution)/shard_map/all_to_all | solution.py:69
  288.0 93.0 %copy-start.6 = (s32[1,3]{1,0:T(1,128)S(1)}, s32[1,3]{1,0:T(1,128)}, u32[]{:S(2)}) copy-start(s32[1,3]{1,0:T(1,128)} %param.19) | copy-start | bytes 40
  288.0 108.7 %all-to-all-start.1 = ((f32[2,1024,128]{2,0,1:T(2,128)}), f32[2,1024,128]{2,0,1:T(2,128)S(1)}, u32[]{:S(2)}, u32[]{:S(2)}) async-start(f32[2,1024,128]{2,0,1:T(2,128)} %copy.145), calls=%async_computation.1 | async-start | bytes 2097152 | tf_op jit(solution)/shard_map/all_to_all | solution.py:75
  380.9 37.0 %copy-start.1 = (f32[94,32]{1,0:T(8,128)}, f32[94,32]{1,0:T(8,128)S(1)}, u32[]{:S(2)}) copy-start(f32[94,32]{1,0:T(8,128)S(1)} %get-tuple-element.481) | copy-start | bytes 36100
  389.9 19.4 %collective-permute-start.3 = (bf16[96,32,128]{2,0,1:T(8,128)(2,1)}, bf16[96,32,128]{2,0,1:T(8,128)(2,1)}, u32[]{:S(2)}, u32[]{:S(2)}) collective-permute-start(bf16[96,32,128]{2,0,1:T(8,128)(2,1)} %get-tuple-element.606), channel_id=1, source_target_pairs={{2,0},{4,2},{6,4},{8,6},{10,8},{12,10},{14,12},{16,14},{18,16},{20... | collective-permute-start | bytes 2359304 | tf_op jit(solution)/shard_map/ppermute | solution.py:29
  391.2 19.3 %collective-permute-start.2 = (bf16[96,32,128]{2,0,1:T(8,128)(2,1)}, bf16[96,32,128]{2,0,1:T(8,128)(2,1)}, u32[]{:S(2)}, u32[]{:S(2)}) collective-permute-start(bf16[96,32,128]{2,0,1:T(8,128)(2,1)} %get-tuple-element.605), channel_id=1, source_target_pairs={{0,2},{2,4},{4,6},{6,8},{8,10},{10,12},{12,14},{14,16},{16,18},{18... | collective-permute-start | bytes 2359304 | tf_op jit(solution)/shard_map/ppermute | solution.py:27
  397.1 19.7 %collective-permute-start.5 = (f32[31,64,128]{2,1,0:T(8,128)S(1)}, f32[31,64,128]{2,1,0:T(8,128)S(1)}, u32[]{:S(2)}, u32[]{:S(2)}) collective-permute-start(f32[31,64,128]{2,1,0:T(8,128)S(1)} %get-tuple-element.614), channel_id=1, source_target_pairs={{1,0},{3,2},{5,4},{7,6},{9,8},{11,10},{13,12},{15,14},{17,16},{19,... | collective-permute-start | bytes 3047432 | tf_op jit(solution)/shard_map/ppermute | solution.py:29
  398.4 19.0 %collective-permute-start.4 = (f32[31,64,128]{2,1,0:T(8,128)S(1)}, f32[31,64,128]{2,1,0:T(8,128)S(1)}, u32[]{:S(2)}, u32[]{:S(2)}) collective-permute-start(f32[31,64,128]{2,1,0:T(8,128)S(1)} %get-tuple-element.613), channel_id=1, source_target_pairs={{0,1},{2,3},{4,5},{6,7},{8,9},{10,11},{12,13},{14,15},{16,17},{18,... | collective-permute-start | bytes 3047432 | tf_op jit(solution)/shard_map/ppermute | solution.py:27
  416.1 1.9 copy-start.3
  422.4 89.9 %all-to-all-start.2 = ((bf16[32,64,128]{2,1,0:T(8,128)(2,1)}), bf16[32,64,128]{2,1,0:T(8,128)(2,1)S(1)}, u32[]{:S(2)}, u32[]{:S(2)}) async-start(bf16[32,64,128]{2,1,0:T(8,128)(2,1)} %convolution_convert_fusion.2), calls=%async_computation.2 | async-start | bytes 1048576 | tf_op jit(solution)/shard_map/all_to_all | solution.py:69
  515.6 21.3 %all-to-all-start.3 = ((f32[2,1024,128]{2,0,1:T(2,128)}), f32[2,1024,128]{2,0,1:T(2,128)S(1)}, u32[]{:S(2)}, u32[]{:S(2)}) async-start(f32[2,1024,128]{2,0,1:T(2,128)} %copy.161), calls=%async_computation.3 | async-start | bytes 2097152 | tf_op jit(solution)/shard_map/all_to_all | solution.py:75
  522.9 161.4 %all-reduce.8.cloned.1.call-start = ((), (), s32[]{:S(2)}) async-start(), calls=%async_computation.8 | async-start | bytes 2097152 | tf_op jit(solution)/shard_map/psum | solution.py:126
  538.3 95.7 %copy-start.5 = (s32[4,8,1]{1,2,0:T(1,128)S(1)}, s32[4,8,1]{1,2,0:T(1,128)}, u32[]{:S(2)}) copy-start(s32[4,8,1]{1,2,0:T(1,128)} %param.21) | copy-start | bytes 388
  538.3 96.0 %collective-permute-start.7 = (f32[31,64,128]{2,1,0:T(8,128)S(1)}, f32[31,64,128]{2,1,0:T(8,128)}, u32[]{:S(2)}, u32[]{:S(2)}) collective-permute-start(f32[31,64,128]{2,1,0:T(8,128)S(1)} %copy.164), channel_id=1, source_target_pairs={{1,0},{3,2},{5,4},{7,6},{9,8},{11,10},{13,12},{15,14},{17,16},{19,... | collective-permute-start | bytes 3047432 | tf_op jit(solution)/shard_map/ppermute | solution.py:29
  541.2 95.0 %collective-permute-start.6 = (f32[31,64,128]{2,1,0:T(8,128)}, f32[31,64,128]{2,1,0:T(8,128)}, u32[]{:S(2)}, u32[]{:S(2)}) collective-permute-start(f32[31,64,128]{2,1,0:T(8,128)} %copy.163), channel_id=1, source_target_pairs={{0,1},{2,3},{4,5},{6,7},{8,9},{10,11},{12,13},{14,15},{16,17},{18,... | collective-permute-start | bytes 3047432 | tf_op jit(solution)/shard_map/ppermute | solution.py:27
  640.9 187.1 %all-reduce.10.cloned.1.call-start = ((), (), s32[]{:S(2)}) async-start(), calls=%async_computation.9 | async-start | bytes 2097152 | tf_op jit(solution)/shard_map/psum | solution.py:126
  724.7 5.1 collective-permute-start.9
  726.0 5.3 collective-permute-start.8
  729.8 2.1 copy-start.2
  729.8 2.1 copy-start.4
  774.2 5.1 collective-permute-start.11
  776.1 5.3 collective-permute-start.10
Sparse Core Ops, SparseCore 0:
  641.0 43.2 all-reduce.7
  785.0 42.9 all-reduce.9
where the time goes:
time: 848 us; the launch traced here: 838 us
  other arithmetic  275 us (32%)
  local copies, waits for them, and re-layouts  269 us (32%)
  waiting for transfers between devices  110 us (13%)
  blocking collectives  69 us (8%)
  starting transfers between devices  64.8 us (8%)
  matrix products  21.8 us (3%)
  between operations  20.4 us (2%)
    add x378, other arithmetic, add_tap(): return summed + jnp.where(offsets == tap_index, kern[tap_index], 0.0)  261 us
    dynamic_slice x378, local copies, waits for them, and re-layouts, add_tap(): return summed + jnp.where(offsets == tap_index, kern[tap_index], 0.0)  244 us
    psum x2, waiting for transfers between devices, on_device(): total = lax.psum(term, 'view')  86.5 us
    all_to_all x2, blocking collectives, along_rows(): return lax.all_to_all(out, 'xy', split_axis=1, concat_axis=0, tiled=True)  36.9 us
    all_to_all x2, blocking collectives, along_rows(): lax.all_to_all(shortened(vol), 'xy', split_axis=0, concat_axis=1, tiled=T...  32.1 us
    ppermute x6, starting transfers between devices, extended(): lax.ppermute(tail, axis, [(i, (i + 1) % count) for i in range(ends)])  24.3 us
    all_to_all x2, starting transfers between devices, along_rows(): lax.all_to_all(shortened(vol), 'xy', split_axis=0, concat_axis=1, tiled=T...  18.1 us
  transfers between devices with their start and end apart: 18, of which 7 were waited for; matrix products, arithmetic and copies ran while one was open for 63% of the time, Pallas kernels for 0%

commit v1 on v0

--- a/solution.py
+++ b/solution.py
@@ -123,7 +123,11 @@
         back = along_rows(back, mats[1][1], half)
         back = along_planes(back, mats[1][3], half)
         term = mine[None] * back
-        total = lax.psum(term, "view")
+
+        def scales_watch(target, comm_axis):
+            return jnp.sum(lax.all_gather(target, comm_axis), 0)
+
+        total = scales_watch(term, "view")
         field = field * total / count[None]
     return field
 

time: 848 us -> 819 us (0.966)
  other arithmetic: 275 us -> 254 us
  local copies, waits for them, and re-layouts: 269 us -> 249 us
    all_gather x0 -> x2, waiting for transfers between devices: none -> 90.3 us  [scales_watch(): return jnp.sum(lax.all_gather(target, comm_axis), 0)]
    psum x2 -> x0, waiting for transfers between devices: 86.5 us -> none  [on_device(): total = lax.psum(term, 'view')]
    add x378, other arithmetic: 261 us -> 236 us  [add_tap(): return summed + jnp.where(offsets == tap_index, kern[tap_index], 0.0)]
    dynamic_slice x378, local copies, waits for them, and re-layouts: 244 us -> 223 us  [add_tap(): return summed + jnp.where(offsets == tap_index, kern[tap_index], 0.0)]
  transfers between devices with their start and end apart: 18 -> 18, of which waited for: 7 -> 7; matrix products, arithmetic and copies ran while one was open for 63% -> 60% of each run, Pallas kernels for 0% -> 0%
where the time goes in v1:
time: 819 us; the launch traced here: 805 us
  other arithmetic  254 us (31%)
  local copies, waits for them, and re-layouts  249 us (30%)
  waiting for transfers between devices  114 us (14%)
  blocking collectives  72.5 us (9%)
  starting transfers between devices  64.7 us (8%)
  matrix products  21.8 us (3%)
  between operations  20.2 us (2%)
  loops' own time  8.38 us (1%)
    add x378, other arithmetic, add_tap(): return summed + jnp.where(offsets == tap_index, kern[tap_index], 0.0)  236 us
    dynamic_slice x378, local copies, waits for them, and re-layouts, add_tap(): return summed + jnp.where(offsets == tap_index, kern[tap_index], 0.0)  223 us
    all_gather x2, waiting for transfers between devices, scales_watch(): return jnp.sum(lax.all_gather(target, comm_axis), 0)  90.3 us
    all_to_all x2, blocking collectives, along_rows(): return lax.all_to_all(out, 'xy', split_axis=1, concat_axis=0, tiled=True)  39 us
    all_to_all x2, blocking collectives, along_rows(): lax.all_to_all(shortened(vol), 'xy', split_axis=0, concat_axis=1, tiled=T...  33.5 us
    ppermute x6, starting transfers between devices, extended(): lax.ppermute(tail, axis, [(i, (i + 1) % count) for i in range(ends)])  23.9 us
    all_to_all x2, starting transfers between devices, along_rows(): lax.all_to_all(shortened(vol), 'xy', split_axis=0, concat_axis=1, tiled=T...  18.1 us
  transfers between devices with their start and end apart: 18, of which 7 were waited for; matrix products, arithmetic and copies ran while one was open for 60% of the time, Pallas kernels for 0%

profile of v1, /device:TPU:0, one launch (start us, length us, event | category | flops | bytes accessed | tf_op | source)
XLA Modules:
  0.0 804.8 jit_solution(8479313486725711573)
XLA Ops:
  6.5 1.5 copy.215
  8.0 1.3 collective-permute-start.1
  9.3 3.9 collective-permute-start
  15.2 74.9 %while.88 = (s32[]{:T(128)}, f32[128,128]{1,0:T(8,128)S(1)}, f32[63]{0:T(128)S(1)}, s32[]{:T(128)}, s32[]{:T(128)}) while((s32[]{:T(128)}, f32[128,128]{1,0:T(8,128)S(1)}, f32[63]{0:T(128)S(1)}, s32[]{:T(128)}, s32[]{:T(128)}) %tuple.181), condition=%wide.region_10.11_spmd.clone, body=%wide.region_9.10_spmd.clone.sunk | while | flops 98307 | bytes 131171 | solution.py:44
  90.1 1.8 fusion.48
  91.9 8.2 %all-to-all-start = ((bf16[32,64,128]{2,1,0:T(8,128)(2,1)}), bf16[32,64,128]{2,1,0:T(8,128)(2,1)S(1)}, u32[]{:S(2)}, u32[]{:S(2)}) async-start(bf16[32,64,128]{2,1,0:T(8,128)(2,1)} %fusion.48), calls=%async_computation | async-start | bytes 1048576 | tf_op jit(solution)/shard_map/all_to_all | solution.py:69
  100.1 80.0 %while.87 = (s32[]{:T(128)}, f32[190,128]{1,0:T(8,128)S(1)}, f32[63]{0:T(128)S(1)}, s32[]{:T(128)}, s32[]{:T(128)}) while((s32[]{:T(128)}, f32[190,128]{1,0:T(8,128)S(1)}, f32[63]{0:T(128)S(1)}, s32[]{:T(128)}, s32[]{:T(128)}) %tuple.184), condition=%wide.region_8.9_spmd.clone, body=%wide.region_7.8_spmd.clone.sunk | while | flops 121603 | bytes 194659 | solution.py:44
  180.2 79.5 %while.89 = (s32[]{:T(128)}, f32[128,128]{1,0:T(8,128)S(1)}, f32[63]{0:T(128)S(1)}, s32[]{:T(128)}, s32[]{:T(128)}) while((s32[]{:T(128)}, f32[128,128]{1,0:T(8,128)S(1)}, f32[63]{0:T(128)S(1)}, s32[]{:T(128)}, s32[]{:T(128)}) %tuple.205), condition=%wide.region_12.13_spmd.clone, body=%wide.region_11.12_spmd.clone.sunk | while | flops 98307 | bytes 131171 | solution.py:44
  261.3 1.8 copy.136
  263.1 7.3 all-to-all-start.1
  270.4 74.3 %while.86 = (s32[]{:T(128)}, f32[94,32]{1,0:T(8,128)S(1)}, f32[63]{0:T(128)S(1)}, s32[]{:T(128)}, s32[]{:T(128)}) while((s32[]{:T(128)}, f32[94,32]{1,0:T(8,128)S(1)}, f32[63]{0:T(128)S(1)}, s32[]{:T(128)}, s32[]{:T(128)}) %tuple.187), condition=%wide.region_6.7_spmd.clone, body=%wide.region_5.6_spmd.clone.sunk | while | flops 15043 | bytes 24163 | solution.py:44
  354.8 5.5 collective-permute-start.2
  360.7 1.3 collective-permute-start.5
  362.0 3.3 collective-permute-start.4
  365.4 1.7 iota_compare_fusion
  367.0 5.9 collective-permute-done.3
  374.2 5.6 fusion.68
  381.6 1.9 convert_divide_fusion.1
  383.6 2.5 convolution_convert_fusion.2
  386.0 10.0 %all-to-all-start.2 = ((bf16[32,64,128]{2,1,0:T(8,128)(2,1)}), bf16[32,64,128]{2,1,0:T(8,128)(2,1)S(1)}, u32[]{:S(2)}, u32[]{:S(2)}) async-start(bf16[32,64,128]{2,1,0:T(8,128)(2,1)} %convolution_convert_fusion.2), calls=%async_computation.2 | async-start | bytes 1048576 | tf_op jit(solution)/shard_map/all_to_all | solution.py:69
  396.0 80.0 %while.85 = (s32[]{:T(128)}, f32[190,128]{1,0:T(8,128)S(1)}, f32[63]{0:T(128)S(1)}, s32[]{:T(128)}, s32[]{:T(128)}) while((s32[]{:T(128)}, f32[190,128]{1,0:T(8,128)S(1)}, f32[63]{0:T(128)S(1)}, s32[]{:T(128)}, s32[]{:T(128)}) %tuple.203), condition=%wide.region_4.5_spmd.clone, body=%wide.region_3.4_spmd.clone.sunk | while | flops 121603 | bytes 194659 | solution.py:44
  477.5 1.8 copy.152
  479.3 7.4 all-to-all-start.3
  486.9 13.8 %all-to-all-done.3 = f32[2,1024,128]{2,0,1:T(2,128)S(1)} async-done(((f32[2,1024,128]{2,0,1:T(2,128)}), f32[2,1024,128]{2,0,1:T(2,128)S(1)}, u32[]{:S(2)}, u32[]{:S(2)}) %all-to-all-start.3) | async-done | bytes 1048608 | tf_op jit(solution)/shard_map/all_to_all | solution.py:75
  503.4 1.5 copy.154
  505.0 4.9 collective-permute-start.6
  509.9 78.9 %while.84 = (s32[]{:T(128)}, f32[94,32]{1,0:T(8,128)S(1)}, f32[63]{0:T(128)S(1)}, s32[]{:T(128)}, s32[]{:T(128)}) while((s32[]{:T(128)}, f32[94,32]{1,0:T(8,128)S(1)}, f32[63]{0:T(128)S(1)}, s32[]{:T(128)}, s32[]{:T(128)}) %tuple.204), condition=%wide.region_2.3_spmd.clone, body=%wide.region_1.2_spmd.clone.sunk | while | flops 15043 | bytes 24163 | solution.py:44
  589.8 1.8 copy.157
  591.6 1.8 copy.156
  593.4 2.9 fusion.42
  596.4 45.5 %all-gather.5.cloned.1.call-done = f32[128,64,128]{2,0,1:T(8,128)} async-done(((f32[32,64,128]{2,0,1:T(8,128)}), f32[128,64,128]{2,0,1:T(8,128)}) %all-gather.5.cloned.1.call-update) | async-done | bytes 4194320 | tf_op jit(solution)/shard_map/all_gather | solution.py:128
  641.8 2.8 reduce_sum.37
  644.7 1.4 fusion.57
  646.1 1.7 convolution_convert_fusion.1
  647.7 18.6 %all_to_all.108 = bf16[32,64,128]{2,1,0:T(8,128)(2,1)S(1)} all-to-all(bf16[32,64,128]{2,1,0:T(8,128)(2,1)S(1)} %convolution_convert_fusion.1), channel_id=1, replica_groups=mesh['view'=4,'xy'=16,'gz'=2] {'xy'}, dimensions={0} | all-to-all | bytes 1048576 | tf_op jit(solution)/shard_map/all_to_all | solution.py:69
  668.6 19.2 %all_to_all.109 = f32[2,1024,128]{2,0,1:T(2,128)S(1)} all-to-all(f32[2,1024,128]{2,0,1:T(2,128)S(1)} %copy.169), channel_id=1, replica_groups=mesh['view'=4,'xy'=16,'gz'=2] {'xy'}, dimensions={1} | all-to-all | bytes 2097152 | tf_op jit(solution)/shard_map/all_to_all | solution.py:75
  689.4 3.2 collective-permute-start.8
  695.4 2.0 convert_divide_fusion
  697.3 1.7 convolution_convert_fusion
  699.0 15.0 %all_to_all.110 = bf16[32,64,128]{2,1,0:T(8,128)(2,1)S(1)} all-to-all(bf16[32,64,128]{2,1,0:T(8,128)(2,1)S(1)} %convolution_convert_fusion), channel_id=1, replica_groups=mesh['view'=4,'xy'=16,'gz'=2] {'xy'}, dimensions={0} | all-to-all | bytes 1048576 | tf_op jit(solution)/shard_map/all_to_all | solution.py:69
  716.3 19.8 %all_to_all.111 = f32[2,1024,128]{2,0,1:T(2,128)S(1)} all-to-all(f32[2,1024,128]{2,0,1:T(2,128)S(1)} %copy.185), channel_id=1, replica_groups=mesh['view'=4,'xy'=16,'gz'=2] {'xy'}, dimensions={1} | all-to-all | bytes 2097152 | tf_op jit(solution)/shard_map/all_to_all | solution.py:75
  737.5 1.3 collective-permute-start.11
  739.4 3.2 collective-permute-start.10
  743.2 1.5 collective-permute-done.10
  745.3 2.9 fusion.36
  748.2 44.9 %all-gather.7.cloned.1.call-done = f32[128,64,128]{2,0,1:T(8,128)} async-done(((f32[32,64,128]{2,0,1:T(8,128)}), f32[128,64,128]{2,0,1:T(8,128)}) %all-gather.7.cloned.1.call-update) | async-done | bytes 4194320 | tf_op jit(solution)/shard_map/all_gather | solution.py:128
  793.1 2.8 reduce_sum.39
  796.2 1.6 copy.192
  (884 shorter events, 488.2 us)
Async XLA Ops:
  6.5 83.6 %copy-start = (f32[32,64,128]{2,1,0:T(8,128)S(1)}, f32[32,64,128]{2,1,0:T(8,128)}, u32[]{:S(2)}) copy-start(f32[32,64,128]{2,1,0:T(8,128)} %param.17) | copy-start | bytes 3145732
  8.0 343.1 %collective-permute-start.1 = (bf16[32,64,128]{2,0,1:T(8,128)(2,1)S(1)}, bf16[32,64,128]{2,0,1:T(8,128)(2,1)S(1)}, u32[]{:S(2)}, u32[]{:S(2)}) collective-permute-start(bf16[32,64,128]{2,0,1:T(8,128)(2,1)S(1)} %bitcast.356), channel_id=1, source_target_pairs={{1,0},{3,2},{5,4},{7,6},{9,8},{11,10},{13,12},{15,14},{17,16},{19,... | collective-permute-start | bytes 1572872 | tf_op jit(solution)/shard_map/ppermute | solution.py:29
  9.3 341.8 %collective-permute-start = (bf16[32,64,128]{2,0,1:T(8,128)(2,1)S(1)}, bf16[32,64,128]{2,0,1:T(8,128)(2,1)}, u32[]{:S(2)}, u32[]{:S(2)}) collective-permute-start(bf16[32,64,128]{2,0,1:T(8,128)(2,1)S(1)} %bitcast.357), channel_id=1, source_target_pairs={{0,1},{2,3},{4,5},{6,7},{8,9},{10,11},{12,13},{14,15},{16,17},{18,... | collective-permute-start | bytes 1572872 | tf_op jit(solution)/shard_map/ppermute | solution.py:27
  91.9 167.8 %all-to-all-start = ((bf16[32,64,128]{2,1,0:T(8,128)(2,1)}), bf16[32,64,128]{2,1,0:T(8,128)(2,1)S(1)}, u32[]{:S(2)}, u32[]{:S(2)}) async-start(bf16[32,64,128]{2,1,0:T(8,128)(2,1)} %fusion.48), calls=%async_computation | async-start | bytes 1048576 | tf_op jit(solution)/shard_map/all_to_all | solution.py:69
  263.1 81.7 %copy-start.8 = (s32[1,3]{1,0:T(1,128)S(1)}, s32[1,3]{1,0:T(1,128)}, u32[]{:S(2)}) copy-start(s32[1,3]{1,0:T(1,128)} %param.19) | copy-start | bytes 40
  263.1 97.2 %all-to-all-start.1 = ((f32[2,1024,128]{2,0,1:T(2,128)}), f32[2,1024,128]{2,0,1:T(2,128)S(1)}, u32[]{:S(2)}, u32[]{:S(2)}) async-start(f32[2,1024,128]{2,0,1:T(2,128)} %copy.136), calls=%async_computation.1 | async-start | bytes 2097152 | tf_op jit(solution)/shard_map/all_to_all | solution.py:75
  344.8 36.8 %copy-start.1 = (f32[94,32]{1,0:T(8,128)}, f32[94,32]{1,0:T(8,128)S(1)}, u32[]{:S(2)}) copy-start(f32[94,32]{1,0:T(8,128)S(1)} %get-tuple-element.481) | copy-start | bytes 36100
  353.6 19.4 %collective-permute-start.3 = (bf16[96,32,128]{2,0,1:T(8,128)(2,1)}, bf16[96,32,128]{2,0,1:T(8,128)(2,1)}, u32[]{:S(2)}, u32[]{:S(2)}) collective-permute-start(bf16[96,32,128]{2,0,1:T(8,128)(2,1)} %get-tuple-element.606), channel_id=1, source_target_pairs={{2,0},{4,2},{6,4},{8,6},{10,8},{12,10},{14,12},{16,14},{18,16},{20... | collective-permute-start | bytes 2359304 | tf_op jit(solution)/shard_map/ppermute | solution.py:29
  354.8 19.3 %collective-permute-start.2 = (bf16[96,32,128]{2,0,1:T(8,128)(2,1)}, bf16[96,32,128]{2,0,1:T(8,128)(2,1)}, u32[]{:S(2)}, u32[]{:S(2)}) collective-permute-start(bf16[96,32,128]{2,0,1:T(8,128)(2,1)} %get-tuple-element.605), channel_id=1, source_target_pairs={{0,2},{2,4},{4,6},{6,8},{8,10},{10,12},{12,14},{14,16},{16,18},{18... | collective-permute-start | bytes 2359304 | tf_op jit(solution)/shard_map/ppermute | solution.py:27
  360.7 19.6 %collective-permute-start.5 = (f32[31,64,128]{2,1,0:T(8,128)S(1)}, f32[31,64,128]{2,1,0:T(8,128)S(1)}, u32[]{:S(2)}, u32[]{:S(2)}) collective-permute-start(f32[31,64,128]{2,1,0:T(8,128)S(1)} %get-tuple-element.614), channel_id=1, source_target_pairs={{1,0},{3,2},{5,4},{7,6},{9,8},{11,10},{13,12},{15,14},{17,16},{19,... | collective-permute-start | bytes 3047432 | tf_op jit(solution)/shard_map/ppermute | solution.py:29
  362.0 19.0 %collective-permute-start.4 = (f32[31,64,128]{2,1,0:T(8,128)S(1)}, f32[31,64,128]{2,1,0:T(8,128)S(1)}, u32[]{:S(2)}, u32[]{:S(2)}) collective-permute-start(f32[31,64,128]{2,1,0:T(8,128)S(1)} %get-tuple-element.613), channel_id=1, source_target_pairs={{0,1},{2,3},{4,5},{6,7},{8,9},{10,11},{12,13},{14,15},{16,17},{18,... | collective-permute-start | bytes 3047432 | tf_op jit(solution)/shard_map/ppermute | solution.py:27
  379.7 1.9 copy-start.3
  386.0 90.0 %all-to-all-start.2 = ((bf16[32,64,128]{2,1,0:T(8,128)(2,1)}), bf16[32,64,128]{2,1,0:T(8,128)(2,1)S(1)}, u32[]{:S(2)}, u32[]{:S(2)}) async-start(bf16[32,64,128]{2,1,0:T(8,128)(2,1)} %convolution_convert_fusion.2), calls=%async_computation.2 | async-start | bytes 1048576 | tf_op jit(solution)/shard_map/all_to_all | solution.py:69
  479.3 7.5 copy-start.7
  479.3 21.4 %all-to-all-start.3 = ((f32[2,1024,128]{2,0,1:T(2,128)}), f32[2,1024,128]{2,0,1:T(2,128)S(1)}, u32[]{:S(2)}, u32[]{:S(2)}) async-start(f32[2,1024,128]{2,0,1:T(2,128)} %copy.152), calls=%async_computation.3 | async-start | bytes 2097152 | tf_op jit(solution)/shard_map/all_to_all | solution.py:75
  486.8 155.1 %all-gather.5.cloned.1.call-start = ((), (), s32[]{:S(2)}) async-start(), calls=%async_computation.8 | async-start | bytes 5242880 | tf_op jit(solution)/shard_map/all_gather | solution.py:128
  502.1 86.7 %copy-start.6 = (s32[4,8,1]{1,2,0:T(1,128)S(1)}, s32[4,8,1]{1,2,0:T(1,128)}, u32[]{:S(2)}) copy-start(s32[4,8,1]{1,2,0:T(1,128)} %param.21) | copy-start | bytes 388
  502.1 87.6 %collective-permute-start.7 = (f32[31,64,128]{2,1,0:T(8,128)S(1)}, f32[31,64,128]{2,1,0:T(8,128)}, u32[]{:S(2)}, u32[]{:S(2)}) collective-permute-start(f32[31,64,128]{2,1,0:T(8,128)S(1)} %copy.155), channel_id=1, source_target_pairs={{1,0},{3,2},{5,4},{7,6},{9,8},{11,10},{13,12},{15,14},{17,16},{19,... | collective-permute-start | bytes 3047432 | tf_op jit(solution)/shard_map/ppermute | solution.py:29
  505.0 86.6 %collective-permute-start.6 = (f32[31,64,128]{2,1,0:T(8,128)}, f32[31,64,128]{2,1,0:T(8,128)}, u32[]{:S(2)}, u32[]{:S(2)}) collective-permute-start(f32[31,64,128]{2,1,0:T(8,128)} %copy.154), channel_id=1, source_target_pairs={{0,1},{2,3},{4,5},{6,7},{8,9},{10,11},{12,13},{14,15},{16,17},{18,... | collective-permute-start | bytes 3047432 | tf_op jit(solution)/shard_map/ppermute | solution.py:27
  596.3 196.8 %all-gather.7.cloned.1.call-start = ((), (), s32[]{:S(2)}) async-start(), calls=%async_computation.9 | async-start | bytes 5242880 | tf_op jit(solution)/shard_map/all_gather | solution.py:128
  688.1 5.1 collective-permute-start.9
  689.4 5.3 collective-permute-start.8
  693.2 2.1 copy-start.2
  693.2 2.1 copy-start.4
  737.5 5.1 collective-permute-start.11
  739.4 5.3 collective-permute-start.10
  793.1 2.8 copy-start.5
Sparse Core Ops, SparseCore 0:
  596.4 45.3 all-gather.4
  748.4 44.6 all-gather.6
